TPU v7x, 32 devices: a whole 2x2x4 slice. The times are simulated.
32 devices in a mesh: expert: 4 (over z), tensor: 8 (over y, x, core).
Axes of the slice: x: 2, y: 2, z: 4, core: 2. Of those that a mesh axis runs over, the one named last changes fastest.
Arguments:
- tokens: bfloat16 [512, 6144], P('expert', 'tensor'), may hold values from -6 to 6
- out_grad: bfloat16 [512, 6144], P('expert', 'tensor'), may hold values from -6 to 6
- expert_ids: int32 [512, 2], P('expert'), may hold values from 0 to 3, all different within a row; in each aligned block of 128 rows (0 to 127, 128 to 255, ...) at most 80 rows name the same one
- route_logits: float32 [512, 2], P('expert'), may hold values from -6 to 6
- w_gate: bfloat16 [4, 6144, 8192], P('expert', 'tensor'), may hold values from -0.078125 to 0.078125
- w_up: bfloat16 [4, 6144, 8192], P('expert', 'tensor'), may hold values from -0.078125 to 0.078125
- w_down: bfloat16 [4, 6144, 8192], P('expert', 'tensor'), may hold values from -0.0625 to 0.0625
- gate_scale: float32 [4, 8192], P('expert', 'tensor'), may hold values from 0.5 to 2
- up_scale: float32 [4, 8192], P('expert', 'tensor'), may hold values from 0.5 to 2
- down_scale: float32 [4, 8192], P('expert', 'tensor'), may hold values from 0.5 to 2
Outputs:
- mixed: bfloat16 [512, 6144], P('expert', 'tensor')
- token_grad: bfloat16 [512, 6144], P('expert', 'tensor')
- logit_grad: float32 [512, 2], P('expert')
- gate_grad: bfloat16 [4, 6144, 8192], P('expert', None, 'tensor')
- up_grad: bfloat16 [4, 6144, 8192], P('expert', None, 'tensor')
- down_grad: bfloat16 [4, 6144, 8192], P('expert', None, 'tensor')
Inputs may be any that keep to these rules, and one draw needn't show every extreme that they name: `expert_ids`: each token names two different experts; among the 128 tokens of one index of the expert axis, each expert is named by at most 80.
All inputs are finite; a program needn't handle non-finite values.
Results may differ from a plain program's by a relative error of at most 0.025.
Values may be sent and summed in bfloat16 or wider, within the bound.
A program may use at most 256 MiB of HBM per device.

v0:
```python
import jax
import jax.numpy as jnp
from jax import lax
from jax.sharding import PartitionSpec as P


def gate_tables(expert_ids, route_logits, count):
    first = jax.nn.sigmoid(route_logits[:, 0] - route_logits[:, 1])
    probs = jnp.stack([first, 1.0 - first], axis=1)
    labels = jnp.arange(count, dtype=jnp.int32)
    chosen = (expert_ids[:, :, None] == labels[None, None, :]).astype(jnp.float32)
    per_expert = jnp.sum(probs[:, :, None] * chosen, axis=1)
    member = jnp.sum(chosen, axis=1)
    return (probs, chosen, per_expert, member)


def contract_rows(left, right):
    return lax.dot_general(
        left, right, (((0,), (0,)), ((), ())), preferred_element_type=jnp.float32
    )


def body(
    tokens,
    out_grad,
    expert_ids,
    route_logits,
    w_gate,
    w_up,
    w_down,
    gate_scale,
    up_scale,
    down_scale,
):
    groups = lax.axis_size("expert")
    local_tokens, feat_width = tokens.shape
    probs, chosen, per_expert, member = gate_tables(expert_ids, route_logits, groups)
    member_cols = member.T.astype(jnp.bfloat16)[:, :, None]
    weight_cols = per_expert.T[:, :, None]

    def unpacking(packed):
        return packed.astype(jnp.float32)

    total_rows = groups * local_tokens
    send_rows = tokens[None] * member_cols
    send_grads = (out_grad.astype(jnp.float32)[None] * weight_cols).astype(jnp.bfloat16)
    got_rows, got_grads = (
        lax.all_to_all(send_rows, "expert", split_axis=0, concat_axis=0, tiled=True),
        lax.all_to_all(send_grads, "expert", split_axis=0, concat_axis=0, tiled=True),
    )
    rows_in, grads_in = (
        lax.all_gather(got_rows.reshape(total_rows, feat_width), "tensor", axis=1, tiled=True),
        lax.all_gather(got_grads.reshape(total_rows, feat_width), "tensor", axis=1, tiled=True),
    )
    gate_all, up_all, down_all = (
        lax.all_to_all(w_gate, "tensor", split_axis=2, concat_axis=1, tiled=True),
        lax.all_to_all(w_up, "tensor", split_axis=2, concat_axis=1, tiled=True),
        lax.all_to_all(w_down, "tensor", split_axis=2, concat_axis=1, tiled=True),
    )
    gate_w = gate_all[0]
    up_w = up_all[0]
    down_w = down_all[0]
    gate_pre = jnp.dot(rows_in, gate_w, preferred_element_type=jnp.float32) * gate_scale[0]
    up_pre = jnp.dot(rows_in, up_w, preferred_element_type=jnp.float32) * up_scale[0]
    sigma = jax.nn.sigmoid(gate_pre)
    active = gate_pre * sigma
    hidden = (active * up_pre * down_scale[0]).astype(jnp.bfloat16)
    out_part = jnp.dot(hidden, down_w.T, preferred_element_type=jnp.float32)
    down_grad = contract_rows(grads_in, hidden).astype(jnp.bfloat16)
    back = jnp.dot(grads_in, down_w, preferred_element_type=jnp.float32) * down_scale[0]
    d_gate = (back * up_pre * sigma * (1.0 + gate_pre * (1.0 - sigma)) * gate_scale[0]).astype(
        jnp.bfloat16
    )
    d_up = (back * active * up_scale[0]).astype(jnp.bfloat16)
    gate_grad = contract_rows(rows_in, d_gate).astype(jnp.bfloat16)
    up_grad = contract_rows(rows_in, d_up).astype(jnp.bfloat16)
    grad_part = jnp.dot(d_gate, gate_w.T, preferred_element_type=jnp.float32) + jnp.dot(
        d_up, up_w.T, preferred_element_type=jnp.float32
    )
    out_sum = lax.psum_scatter(
        out_part.astype(jnp.bfloat16), "tensor", scatter_dimension=1, tiled=True
    )
    out_back = lax.all_to_all(
        out_sum.reshape(groups, local_tokens, feat_width),
        "expert",
        split_axis=0,
        concat_axis=0,
        tiled=True,
    )
    grad_sum = lax.psum_scatter(
        grad_part.astype(jnp.bfloat16), "tensor", scatter_dimension=1, tiled=True
    )
    grad_back = lax.all_to_all(
        grad_sum.reshape(groups, local_tokens, feat_width),
        "expert",
        split_axis=0,
        concat_axis=0,
        tiled=True,
    )
    out_float = unpacking(out_back)
    grad_float = unpacking(grad_back)
    mixed = jnp.sum(weight_cols * out_float, axis=0).astype(jnp.bfloat16)
    token_grad = jnp.sum(grad_float, axis=0).astype(jnp.bfloat16)
    local_score = jnp.einsum("td,etd->te", out_grad.astype(jnp.float32), out_float)
    score = lax.psum(local_score, "tensor")
    pick = jnp.sum(chosen * score[:, None, :], axis=2)
    mean_pick = jnp.sum(probs * pick, axis=1, keepdims=True)
    logit_grad = probs * (pick - mean_pick)
    return (mixed, token_grad, logit_grad, gate_grad[None], up_grad[None], down_grad[None])


def solution(mesh):
    in_specs = (
        P("expert", "tensor"),
        P("expert", "tensor"),
        P("expert", None),
        P("expert", None),
        P("expert", "tensor", None),
        P("expert", "tensor", None),
        P("expert", "tensor", None),
        P("expert", "tensor"),
        P("expert", "tensor"),
        P("expert", "tensor"),
    )
    out_specs = (
        P("expert", "tensor"),
        P("expert", "tensor"),
        P("expert", None),
        P("expert", None, "tensor"),
        P("expert", None, "tensor"),
        P("expert", None, "tensor"),
    )
    return jax.shard_map(body, mesh=mesh, in_specs=in_specs, out_specs=out_specs, check_vma=False)
```

profile of v0, /device:TPU:0, one launch (start us, length us, event | category | flops | bytes accessed | tf_op | source)
XLA Modules:
  0.0 1169.5 jit_solution(9757918283287078089)
XLA Ops:
  7.2 0.7 convert_reduce_fusion
  7.9 1.9 broadcast_multiply_fusion
  9.8 6.3 all-to-all-start
  16.1 51.2 %copy.36 = bf16[1,768,8192]{1,0,2:T(2,128)(2,1)} copy(bf16[1,768,8192]{2,1,0:T(8,128)(2,1)} %param.14) | data formatting | bytes 25165824 | tf_op args[4]
  67.4 0.5 broadcast.37
  67.9 126.8 %reduce.1 = bf16[8192,768]{1,0:T(8,128)(2,1)} reduce(bf16[8192,1,768]{2,1,0:T(2,128)(2,1)} %bitcast.55, bf16[]{:T(256)} %broadcast.37), dimensions={1}, to_apply=%bitcast.33.reduce_sub_computation | reduce | bytes 25165826
  194.7 12.3 %reshape.43 = bf16[8,2,393216]{2,1,0:T(2,128)(2,1)} reshape(bf16[8192,768]{1,0:T(8,128)(2,1)} %reduce.1) | data formatting | bytes 25165824
  207.0 0.0 all-to-all-done
  207.0 0.9 copy-done
  207.9 5.6 all-to-all-start.1
  213.4 51.2 %copy.38 = bf16[1,768,8192]{1,0,2:T(2,128)(2,1)} copy(bf16[1,768,8192]{2,1,0:T(8,128)(2,1)} %param.15) | data formatting | bytes 25165824 | tf_op args[5]
  264.7 126.8 %reduce.2 = bf16[8192,768]{1,0:T(8,128)(2,1)} reduce(bf16[8192,1,768]{2,1,0:T(2,128)(2,1)} %bitcast.60, bf16[]{:T(256)} %broadcast.37), dimensions={1}, to_apply=%bitcast.31.reduce_sub_computation | reduce | bytes 25165826
  391.5 12.3 %reshape.41 = bf16[8,2,393216]{2,1,0:T(2,128)(2,1)} reshape(bf16[8192,768]{1,0:T(8,128)(2,1)} %reduce.2) | data formatting | bytes 25165824
  403.7 0.0 all-to-all-done.1
  403.7 5.5 all-to-all-start.2
  409.3 51.2 %copy.40 = bf16[1,768,8192]{1,0,2:T(2,128)(2,1)} copy(bf16[1,768,8192]{2,1,0:T(8,128)(2,1)} %param.16) | data formatting | bytes 25165824 | tf_op args[6]
  460.5 126.8 %reduce.3 = bf16[8192,768]{1,0:T(8,128)(2,1)} reduce(bf16[8192,1,768]{2,1,0:T(2,128)(2,1)} %bitcast.56, bf16[]{:T(256)} %broadcast.37), dimensions={1}, to_apply=%bitcast.35.reduce_sub_computation | reduce | bytes 25165826
  587.3 12.3 %reshape.45 = bf16[8,2,393216]{2,1,0:T(2,128)(2,1)} reshape(bf16[8192,768]{1,0:T(8,128)(2,1)} %reduce.3) | data formatting | bytes 25165824
  599.6 0.0 all-to-all-done.2
  599.6 5.3 all-to-all-start.3
  604.9 0.0 all-gather.3.cloned.1.call-start
  605.0 0.7 all-gather.3.cloned.1.call-update
  605.7 0.3 reduce-scatter.3.cloned.1.call-start
  606.0 18.0 %reshape.44 = bf16[8192,1,768]{2,1,0:T(2,128)(2,1)} reshape(bf16[8,2,393216]{2,1,0:T(2,128)(2,1)} %all-to-all-done.1) | data formatting | bytes 25165824
  623.9 15.1 %copy.45 = bf16[1,768,8192]{1,2,0:T(8,128)(2,1)} copy(bf16[1,768,8192]{1,0,2:T(2,128)(2,1)} %bitcast.57) | data formatting | bytes 25165824
  639.0 16.6 %copy.37 = bf16[1,8,768,1024]{3,2,1,0:T(8,128)(2,1)} copy(bf16[1,8,768,1024]{2,3,1,0:T(8,128)(2,1)} %bitcast.61) | data formatting | bytes 25165824 | tf_op jit(solution)/shard_map/all_to_all | solution.py:56
  655.6 18.1 %reshape.42 = bf16[8192,1,768]{2,1,0:T(2,128)(2,1)} reshape(bf16[8,2,393216]{2,1,0:T(2,128)(2,1)} %all-to-all-done.2) | data formatting | bytes 25165824
  673.7 15.1 %copy.46 = bf16[1,768,8192]{1,2,0:T(8,128)(2,1)} copy(bf16[1,768,8192]{1,0,2:T(2,128)(2,1)} %bitcast.58) | data formatting | bytes 25165824
  688.7 16.6 %copy.39 = bf16[1,8,768,1024]{3,2,1,0:T(8,128)(2,1)} copy(bf16[1,8,768,1024]{2,3,1,0:T(8,128)(2,1)} %bitcast.62) | data formatting | bytes 25165824 | tf_op jit(solution)/shard_map/all_to_all | solution.py:57
  705.3 63.9 %all-to-all-done.3 = bf16[8,2,393216]{2,1,0:T(2,128)(2,1)} async-done(((bf16[8,2,393216]{2,1,0:T(2,128)(2,1)}), bf16[8,2,393216]{2,1,0:T(2,128)(2,1)}, u32[]{:S(2)}, u32[]{:S(2)}) %all-to-all-start.3) | async-done | bytes 12582944 | tf_op jit(solution)/shard_map/all_to_all | solution.py:58
  769.2 17.9 %reshape.46 = bf16[8192,1,768]{2,1,0:T(2,128)(2,1)} reshape(bf16[8,2,393216]{2,1,0:T(2,128)(2,1)} %all-to-all-done.3) | data formatting | bytes 25165824
  787.1 15.1 %copy.47 = bf16[1,768,8192]{1,2,0:T(8,128)(2,1)} copy(bf16[1,768,8192]{1,0,2:T(2,128)(2,1)} %bitcast.59) | data formatting | bytes 25165824
  802.2 16.6 %copy.41 = bf16[1,8,768,1024]{3,2,1,0:T(8,128)(2,1)} copy(bf16[1,8,768,1024]{2,3,1,0:T(8,128)(2,1)} %bitcast.63) | data formatting | bytes 25165824 | tf_op jit(solution)/shard_map/all_to_all | solution.py:58
  818.9 0.0 copy-start.7
  818.9 0.0 slice-start
  818.9 13.5 %fusion.4 = f32[512,1024]{1,0:T(8,128)S(1)} fusion(bf16[512,6144]{1,0:T(8,128)(2,1)} %all-gather.3.cloned.1.call-done, bf16[6144,1024]{1,0:T(8,128)(2,1)} %bitcast.64), kind=kOutput, calls=%fused_computation.26 | convolution fusion | flops 6442450944 | bytes 20971520 | tf_op jit(solution)/shard_map/dot_general | solution.py:63
  832.5 0.0 slice-start.2
  832.5 11.8 %multiply_convert_fusion.2 = (bf16[512,1024]{1,0:T(8,128)(2,1)S(1)}, f32[512,1024]{1,0:T(8,128)}) fusion(f32[1024]{0:T(1024)S(1)} %bitcast.82, f32[1024]{0:T(1024)S(1)} %bitcast.84, f32[512,1024]{1,0:T(8,128)S(1)} %fusion.4, f32[1024]{0:T(1024)S(1)} %bitcast.86, bf16[512,6144]{1,0:T(8,128)(2,1)S(1)} %copy-done.4, bf16[6144,1024]{1,0:T(8,128)(2,1)} %bitcast.66), kind=kOutput, calls=%fused_computation.7 | convolution fusion | flops 6447169536 | bytes 24129536 | tf_op jit(solution)/shard_map/dot_general | solution.py:64
  844.3 1.0 copy-done.10
  845.3 8.6 convolution_convert_fusion
  853.9 0.0 reduce-scatter.3.cloned.1.call-update
  853.9 61.4 %reduce-scatter.3.cloned.1.call-done = bf16[512,768]{1,0:T(8,128)(2,1)} async-done(((bf16[512,6144]{1,0:T(8,128)(2,1)}), bf16[512,768]{1,0:T(8,128)(2,1)}) %reduce-scatter.3.cloned.1.call-update) | async-done | bytes 786448 | tf_op jit(solution)/shard_map/reduce_scatter | solution.py:80
  915.3 4.6 all-to-all-start.4
  920.0 19.9 %all-to-all-done.4 = bf16[4,128,768]{2,1,0:T(8,128)(2,1)S(1)} async-done(((bf16[4,128,768]{2,1,0:T(8,128)(2,1)}), bf16[4,128,768]{2,1,0:T(8,128)(2,1)S(1)}, u32[]{:S(2)}, u32[]{:S(2)}) %all-to-all-start.4) | async-done | bytes 786464 | tf_op jit(solution)/shard_map/all_to_all | solution.py:83
  939.8 1.0 fusion.1
  940.9 0.1 copy.44
  940.9 12.0 %psum.7 = f32[128,4]{0,1:T(4,128)S(1)} all-reduce(f32[128,4]{0,1:T(4,128)S(1)} %bitcast.78), channel_id=1, replica_groups=mesh['expert'=4,'tensor'=8] {'tensor'}, use_global_device_ids=true, to_apply=%region_6.0 | all-reduce | flops 512 | bytes 4096 | tf_op jit(solution)/shard_map/psum | solution.py:105
  953.0 1.0 multiply_convert_fusion.3
  953.9 23.3 %all_to_all.65 = bf16[4,128,768]{2,1,0:T(8,128)(2,1)} all-to-all(bf16[4,128,768]{2,1,0:T(8,128)(2,1)S(1)} %get-tuple-element.12), channel_id=1, replica_groups=mesh['expert'=4,'tensor'=8] {'expert'}, dimensions={0} | all-to-all | bytes 1572864 | tf_op jit(solution)/shard_map/all_to_all | solution.py:49
  977.3 0.0 all-gather.5.cloned.1.call-update
  977.3 0.0 reduce-scatter.5.cloned.1.call-start
  977.3 43.5 %all-gather.5.cloned.1.call-done = bf16[512,6144]{1,0:T(8,128)(2,1)} async-done(((bf16[512,768]{1,0:T(8,128)(2,1)}), bf16[512,6144]{1,0:T(8,128)(2,1)}) %all-gather.5.cloned.1.call-update) | async-done | bytes 6291472 | tf_op jit(solution)/shard_map/all_gather | solution.py:53
  1020.8 14.3 %multiply_convert_fusion = (bf16[512,1024]{1,0:T(8,128)(2,1)S(1)}, bf16[512,1024]{1,0:T(8,128)(2,1)S(1)}) fusion(f32[1024]{0:T(1024)S(1)} %bitcast.83, f32[1024]{0:T(1024)S(1)} %bitcast.85, f32[512,1024]{1,0:T(8,128)} %copy-done.12, f32[1024]{0:T(1024)S(1)} %bitcast.87, f32[512,1024]{1,0:T(8,128)} %get-tuple-element.15, ...), kind=kOutput, calls=%fused_computation.5 | convolution fusion | flops 6451888128 | bytes 25178112 | tf_op jit(solution)/shard_map/dot_general | solution.py:70
  1035.1 20.2 %fusion.5 = f32[512,6144]{1,0:T(8,128)} fusion(bf16[512,1024]{1,0:T(8,128)(2,1)S(1)} %get-tuple-element.11, bf16[6144,1024]{1,0:T(8,128)(2,1)} %bitcast.65), kind=kOutput, calls=%fused_computation.27 | convolution fusion | flops 6442450944 | bytes 26214400 | tf_op jit(solution)/shard_map/dot_general | solution.py:77
  1055.4 20.3 %add_convert_fusion = bf16[512,6144]{1,0:T(8,128)(2,1)} fusion(f32[512,6144]{1,0:T(8,128)} %fusion.5, bf16[512,1024]{1,0:T(8,128)(2,1)S(1)} %get-tuple-element.10, bf16[6144,1024]{1,0:T(8,128)(2,1)} %bitcast.67), kind=kOutput, calls=%fused_computation.3 | convolution fusion | flops 6448742400 | bytes 32505856 | tf_op jit(solution)/shard_map/dot_general | solution.py:77
  1075.6 0.0 reduce-scatter.5.cloned.1.call-update
  1075.7 0.6 subtract_multiply_fusion
  1076.3 12.6 %convert_bitcast_fusion.1 = bf16[1,6144,1024]{2,1,0:T(8,128)(2,1)} fusion(bf16[512,6144]{1,0:T(8,128)(2,1)} %all-gather.3.cloned.1.call-done, bf16[512,1024]{1,0:T(8,128)(2,1)} %copy-done.11), kind=kOutput, calls=%fused_computation.1 | convolution fusion | flops 6448742400 | bytes 19922944 | tf_op jit(solution)/shard_map/dot_general | solution.py:18
  1088.8 9.8 convert_bitcast_fusion.2
  1098.7 38.8 %reduce-scatter.5.cloned.1.call-done = bf16[512,768]{1,0:T(8,128)(2,1)} async-done(((bf16[512,6144]{1,0:T(8,128)(2,1)}), bf16[512,768]{1,0:T(8,128)(2,1)}) %reduce-scatter.5.cloned.1.call-update) | async-done | bytes 786448 | tf_op jit(solution)/shard_map/reduce_scatter | solution.py:90
  1137.4 4.6 all-to-all-start.6
  1142.0 11.8 %convert_bitcast_fusion = bf16[1,6144,1024]{2,1,0:T(8,128)(2,1)} fusion(bf16[512,6144]{1,0:T(8,128)(2,1)} %all-gather.5.cloned.1.call-done, bf16[512,1024]{1,0:T(8,128)(2,1)} %copy-done.10), kind=kOutput, calls=%fused_computation | convolution fusion | flops 6448742400 | bytes 19922944 | tf_op jit(solution)/shard_map/dot_general | solution.py:18
  1153.9 8.1 all-to-all-done.6
  1162.0 0.8 reduce_sum.60
  (40 shorter events, 0.2 us)
Async XLA Ops:
  9.8 197.2 %all-to-all-start = ((bf16[4,128,768]{2,1,0:T(8,128)(2,1)}), bf16[4,128,768]{2,1,0:T(8,128)(2,1)S(1)}, u32[]{:S(2)}, u32[]{:S(2)}) async-start(bf16[4,128,768]{2,1,0:T(8,128)(2,1)} %broadcast_multiply_fusion), calls=%async_computation | async-start | bytes 1572864 | tf_op jit(solution)/shard_map/all_to_all | solution.py:48
  207.0 0.9 copy-start
  207.9 195.9 %all-to-all-start.1 = ((bf16[8,2,393216]{2,1,0:T(2,128)(2,1)}), bf16[8,2,393216]{2,1,0:T(2,128)(2,1)}, u32[]{:S(2)}, u32[]{:S(2)}) async-start(bf16[8,2,393216]{2,1,0:T(2,128)(2,1)} %reshape.43), calls=%async_computation.1 | async-start | bytes 25165824 | tf_op jit(solution)/shard_map/all_to_all | solution.py:56
  403.7 195.9 %all-to-all-start.2 = ((bf16[8,2,393216]{2,1,0:T(2,128)(2,1)}), bf16[8,2,393216]{2,1,0:T(2,128)(2,1)}, u32[]{:S(2)}, u32[]{:S(2)}) async-start(bf16[8,2,393216]{2,1,0:T(2,128)(2,1)} %reshape.41), calls=%async_computation.2 | async-start | bytes 25165824 | tf_op jit(solution)/shard_map/all_to_all | solution.py:57
  599.6 169.6 %all-to-all-start.3 = ((bf16[8,2,393216]{2,1,0:T(2,128)(2,1)}), bf16[8,2,393216]{2,1,0:T(2,128)(2,1)}, u32[]{:S(2)}, u32[]{:S(2)}) async-start(bf16[8,2,393216]{2,1,0:T(2,128)(2,1)} %reshape.45), calls=%async_computation.3 | async-start | bytes 25165824 | tf_op jit(solution)/shard_map/all_to_all | solution.py:58
  604.9 213.9 %all-gather.3.cloned.1.call-start = ((), (), s32[]{:S(2)}) async-start(), calls=%async_computation.9 | async-start | bytes 7077888 | tf_op jit(solution)/shard_map/all_gather | solution.py:52
  605.7 309.6 %reduce-scatter.3.cloned.1.call-start = ((), (), s32[]{:S(2)}) async-start(), calls=%async_computation.10 | async-start | bytes 7077888 | tf_op jit(solution)/shard_map/reduce_scatter | solution.py:80
  818.8 13.6 %copy-start.4 = (bf16[512,6144]{1,0:T(8,128)(2,1)S(1)}, bf16[512,6144]{1,0:T(8,128)(2,1)}, u32[]{:S(2)}) copy-start(bf16[512,6144]{1,0:T(8,128)(2,1)} %all-gather.3.cloned.1.call-done) | copy-start | bytes 18874372
  818.8 13.6 %copy-start.5 = (f32[1,1024]{1,0:T(1,128)S(1)}, f32[1,1024]{1,0:T(1,128)}, u32[]{:S(2)}) copy-start(f32[1,1024]{1,0:T(1,128)} %param.19) | copy-start | bytes 12292
  818.8 13.6 %copy-start.6 = (f32[1,1024]{1,0:T(1,128)S(1)}, f32[1,1024]{1,0:T(1,128)}, u32[]{:S(2)}) copy-start(f32[1,1024]{1,0:T(1,128)} %param.18) | copy-start | bytes 12292
  818.9 13.6 %copy-start.7 = (f32[1,1024]{1,0:T(1,128)S(1)}, f32[1,1024]{1,0:T(1,128)}, u32[]{:S(2)}) copy-start(f32[1,1024]{1,0:T(1,128)} %param.17) | copy-start | bytes 12292
  818.9 26.4 %slice-start = ((s8[12582912]{0:T(1024)(128)(4,1)}), s8[4194304]{0:T(1024)(128)(4,1)S(1)}, s32[]{:S(2)}) async-start(s8[12582912]{0:T(1024)(128)(4,1)} %bitcast.69), calls=%async_computation.13 | async-start | bytes 8388608
  818.9 26.4 %slice-start.1 = ((s8[12582912]{0:T(1024)(128)(4,1)}), s8[4194304]{0:T(1024)(128)(4,1)S(1)}, s32[]{:S(2)}) async-start(s8[12582912]{0:T(1024)(128)(4,1)} %bitcast.69), calls=%async_computation.14 | async-start | bytes 8388608
  832.4 11.8 %copy-start.12 = (f32[512,1024]{1,0:T(8,128)}, f32[512,1024]{1,0:T(8,128)S(1)}, u32[]{:S(2)}) copy-start(f32[512,1024]{1,0:T(8,128)S(1)} %fusion.4) | copy-start | bytes 6291460
  832.5 12.8 %slice-start.2 = ((s8[12582912]{0:T(1024)(128)(4,1)}), s8[4194304]{0:T(1024)(128)(4,1)S(1)}, s32[]{:S(2)}) async-start(s8[12582912]{0:T(1024)(128)(4,1)} %bitcast.69), calls=%async_computation.15 | async-start | bytes 8388608
  844.2 1.0 copy-start.10
  853.9 66.0 %copy-start.1 = (bf16[128,768]{1,0:T(8,128)(2,1)S(1)}, bf16[128,768]{1,0:T(8,128)(2,1)}, u32[]{:S(2)}) copy-start(bf16[128,768]{1,0:T(8,128)(2,1)} %param.11) | copy-start | bytes 589828
  853.9 66.0 %copy-start.3 = (f32[128,2]{0,1:T(2,128)S(1)}, f32[128,2]{0,1:T(2,128)}, u32[]{:S(2)}) copy-start(f32[128,2]{0,1:T(2,128)} %param.13) | copy-start | bytes 3076
  853.9 99.0 %copy-start.2 = (s32[128,2]{0,1:T(2,128)S(1)}, s32[128,2]{0,1:T(2,128)}, u32[]{:S(2)}) copy-start(s32[128,2]{0,1:T(2,128)} %param.12) | copy-start | bytes 3076
  915.3 24.5 %all-to-all-start.4 = ((bf16[4,128,768]{2,1,0:T(8,128)(2,1)}), bf16[4,128,768]{2,1,0:T(8,128)(2,1)S(1)}, u32[]{:S(2)}, u32[]{:S(2)}) async-start(bf16[4,128,768]{2,1,0:T(8,128)(2,1)} %bitcast.75), calls=%async_computation.5 | async-start | bytes 1572864 | tf_op jit(solution)/shard_map/all_to_all | solution.py:83
  919.9 100.9 %all-gather.5.cloned.1.call-start = ((), (), s32[]{:S(2)}) async-start(), calls=%async_computation.11 | async-start | bytes 7077888 | tf_op jit(solution)/shard_map/all_gather | solution.py:53
  977.3 160.1 %reduce-scatter.5.cloned.1.call-start = ((), (), s32[]{:S(2)}) async-start(), calls=%async_computation.12 | async-start | bytes 7077888 | tf_op jit(solution)/shard_map/reduce_scatter | solution.py:90
  1035.1 20.2 %copy-start.8 = (bf16[512,1024]{1,0:T(8,128)(2,1)}, bf16[512,1024]{1,0:T(8,128)(2,1)S(1)}, u32[]{:S(2)}) copy-start(bf16[512,1024]{1,0:T(8,128)(2,1)S(1)} %get-tuple-element.11) | copy-start | bytes 3145732
  1035.1 20.2 %copy-start.11 = (bf16[512,1024]{1,0:T(8,128)(2,1)}, bf16[512,1024]{1,0:T(8,128)(2,1)S(1)}, u32[]{:S(2)}) copy-start(bf16[512,1024]{1,0:T(8,128)(2,1)S(1)} %get-tuple-element.10) | copy-start | bytes 3145732
  1075.6 13.2 %slice-start.3 = ((s8[6291456]{0:T(1024)(128)(4,1)}), s8[2097152]{0:T(1024)(128)(4,1)S(1)}, s32[]{:S(2)}) async-start(s8[6291456]{0:T(1024)(128)(4,1)} %bitcast.80), calls=%async_computation.16 | async-start | bytes 4194304
  1076.2 12.6 %slice-start.4 = ((s8[6291456]{0:T(1024)(128)(4,1)}), s8[4194304]{0:T(1024)(128)(4,1)S(1)}, s32[]{:S(2)}) async-start(s8[6291456]{0:T(1024)(128)(4,1)} %bitcast.80), calls=%async_computation.17 | async-start | bytes 8388608
  1076.2 12.6 %copy-start.9 = (bf16[512,1024]{1,0:T(8,128)(2,1)S(1)}, bf16[512,1024]{1,0:T(8,128)(2,1)}, u32[]{:S(2)}) copy-start(bf16[512,1024]{1,0:T(8,128)(2,1)} %copy-done.8) | copy-start | bytes 3145732
  1137.4 24.5 %all-to-all-start.6 = ((bf16[4,128,768]{2,1,0:T(8,128)(2,1)}), bf16[4,128,768]{2,1,0:T(8,128)(2,1)S(1)}, u32[]{:S(2)}, u32[]{:S(2)}) async-start(bf16[4,128,768]{2,1,0:T(8,128)(2,1)} %bitcast.74), calls=%async_computation.8 | async-start | bytes 1572864 | tf_op jit(solution)/shard_map/all_to_all | solution.py:93
Sparse Core Ops, SparseCore 0:
  607.6 112.5 all-gather.2
  854.0 61.2 reduce-scatter.2
  977.4 43.3 all-gather.4
  1075.8 61.6 reduce-scatter.4
where the time goes:
time: 1180 us; the launch traced here: 1170 us
  other arithmetic  385 us (33%)
  local copies, waits for them, and re-layouts  342 us (29%)
  waiting for transfers between devices  236 us (20%)
  matrix products  124 us (11%)
  blocking collectives  35.3 us (3%)
  starting transfers between devices  32.3 us (3%)
  between operations  14.2 us (1%)
    unnamed x5, other arithmetic  380 us
    unnamed x49, local copies, waits for them, and re-layouts  292 us
    all_to_all x1, waiting for transfers between devices, body(): lax.all_to_all(w_down, 'tensor', split_axis=2, concat_axis=1, tiled=True)  63.9 us
    reduce_scatter x1, waiting for transfers between devices, body(): lax.psum_scatter(out_part.astype(jnp.bfloat16), 'tensor', scatter_dimensi...  61.4 us
    all_gather x1, waiting for transfers between devices, body(): lax.all_gather(got_grads.reshape(total_rows, feat_width), 'tensor', axis=...  43.5 us
    reduce_scatter x1, waiting for transfers between devices, body(): lax.psum_scatter(grad_part.astype(jnp.bfloat16), 'tensor', scatter_dimens...  38.8 us
    dot_general x3, matrix products, contract_rows(): lax.dot_general(left, right, (((0,), (0,)), ((), ())), preferred_element_...  34.2 us
  transfers between devices with their start and end apart: 10, of which 6 were waited for; matrix products, arithmetic and copies ran while one was open for 65% of the time, Pallas kernels for 0%

commit v1 on v0

--- a/solution.py
+++ b/solution.py
@@ -55,7 +55,12 @@
     gate_all, up_all, down_all = (
         lax.all_to_all(w_gate, "tensor", split_axis=2, concat_axis=1, tiled=True),
         lax.all_to_all(w_up, "tensor", split_axis=2, concat_axis=1, tiled=True),
-        lax.all_to_all(w_down, "tensor", split_axis=2, concat_axis=1, tiled=True),
+        jnp.concatenate(
+            lax.all_to_all(
+                jnp.stack(jnp.split(w_down, lax.axis_size("tensor"), axis=2)), "tensor", 0, 0
+            ),
+            axis=1,
+        ),
     )
     gate_w = gate_all[0]
     up_w = up_all[0]

time: 1180 us -> 1060 us (0.90)
  other arithmetic: 385 us -> 259 us
  waiting for transfers between devices: 236 us -> 332 us
  local copies, waits for them, and re-layouts: 342 us -> 251 us
    all_to_all x1, waiting for transfers between devices: 0.01 us -> 142 us  [body(): lax.all_to_all(w_up, 'tensor', split_axis=2, concat_axis=1, tiled=True)]
    unnamed x5 -> x3, other arithmetic: 380 us -> 254 us
    unnamed x49 -> x48, local copies, waits for them, and re-layouts: 292 us -> 215 us
    all_to_all x1, waiting for transfers between devices: 63.9 us -> 18 us  [body(): lax.all_to_all(jnp.stack(jnp.split(w_down, lax.axis_size('tensor'), axis=...]
    all_to_all x1 -> x0, local copies, waits for them, and re-layouts: 16.6 us -> none  [body(): lax.all_to_all(w_down, 'tensor', split_axis=2, concat_axis=1, tiled=True)]
  transfers between devices with their start and end apart: 10 -> 10, of which waited for: 6 -> 7; matrix products, arithmetic and copies ran while one was open for 65% -> 53% of each run, Pallas kernels for 0% -> 0%
where the time goes in v1:
time: 1060 us; the launch traced here: 1050 us
  waiting for transfers between devices  332 us (31%)
  other arithmetic  259 us (24%)
  local copies, waits for them, and re-layouts  251 us (24%)
  matrix products  129 us (12%)
  blocking collectives  35.3 us (3%)
  starting transfers between devices  32.4 us (3%)
  between operations  14.1 us (1%)
    unnamed x3, other arithmetic  254 us
    unnamed x48, local copies, waits for them, and re-layouts  215 us
    all_to_all x1, waiting for transfers between devices, body(): lax.all_to_all(w_up, 'tensor', split_axis=2, concat_axis=1, tiled=True)  142 us
    reduce_scatter x1, waiting for transfers between devices, body(): lax.psum_scatter(out_part.astype(jnp.bfloat16), 'tensor', scatter_dimensi...  61.4 us
    all_gather x1, waiting for transfers between devices, body(): lax.all_gather(got_grads.reshape(total_rows, feat_width), 'tensor', axis=...  43.5 us
    reduce_scatter x1, waiting for transfers between devices, body(): lax.psum_scatter(grad_part.astype(jnp.bfloat16), 'tensor', scatter_dimens...  38.8 us
    dot_general x3, matrix products, contract_rows(): lax.dot_general(left, right, (((0,), (0,)), ((), ())), preferred_element_...  34.2 us
    all_to_all x1, blocking collectives, body(): lax.all_to_all(send_grads, 'expert', split_axis=0, concat_axis=0, tiled=T...  23.4 us
  transfers between devices with their start and end apart: 10, of which 7 were waited for; matrix products, arithmetic and copies ran while one was open for 53% of the time, Pallas kernels for 0%

profile of v1, /device:TPU:0, one launch (start us, length us, event | category | flops | bytes accessed | tf_op | source)
XLA Modules:
  0.0 1052.7 jit_solution(350164132859021554)
XLA Ops:
  7.2 0.7 convert_reduce_fusion
  7.9 1.9 broadcast_multiply_fusion
  9.8 6.3 all-to-all-start
  16.1 51.2 %copy.32 = bf16[1,768,8192]{1,0,2:T(2,128)(2,1)} copy(bf16[1,768,8192]{2,1,0:T(8,128)(2,1)} %param.14) | data formatting | bytes 25165824 | tf_op args[4]
  67.4 0.5 broadcast.37
  67.9 126.8 %reduce.1 = bf16[8192,768]{1,0:T(8,128)(2,1)} reduce(bf16[8192,1,768]{2,1,0:T(2,128)(2,1)} %bitcast.66, bf16[]{:T(256)} %broadcast.37), dimensions={1}, to_apply=%bitcast.46.reduce_sub_computation | reduce | bytes 25165826
  194.7 12.3 %reshape.42 = bf16[8,2,393216]{2,1,0:T(2,128)(2,1)} reshape(bf16[8192,768]{1,0:T(8,128)(2,1)} %reduce.1) | data formatting | bytes 25165824
  207.0 0.9 copy-done.1
  207.9 5.9 all-to-all-start.1
  213.8 51.2 %copy.34 = bf16[1,768,8192]{1,0,2:T(2,128)(2,1)} copy(bf16[1,768,8192]{2,1,0:T(8,128)(2,1)} %param.15) | data formatting | bytes 25165824 | tf_op args[5]
  265.1 126.8 %reduce.2 = bf16[8192,768]{1,0:T(8,128)(2,1)} reduce(bf16[8192,1,768]{2,1,0:T(2,128)(2,1)} %bitcast.67, bf16[]{:T(256)} %broadcast.37), dimensions={1}, to_apply=%bitcast.44.reduce_sub_computation | reduce | bytes 25165826
  391.8 12.3 %reshape.40 = bf16[8,2,393216]{2,1,0:T(2,128)(2,1)} reshape(bf16[8192,768]{1,0:T(8,128)(2,1)} %reduce.2) | data formatting | bytes 25165824
  404.1 0.0 all-to-all-done.1
  404.1 5.3 all-to-all-start.2
  409.5 0.0 all-gather.3.cloned.1.call-start
  409.5 0.7 all-gather.3.cloned.1.call-update
  410.2 2.7 bitcast_dynamic-update-slice_fusion.7
  412.9 2.7 bitcast_dynamic-update-slice_fusion.6
  415.6 2.7 bitcast_dynamic-update-slice_fusion.5
  418.3 2.7 bitcast_dynamic-update-slice_fusion.4
  421.0 2.8 bitcast_dynamic-update-slice_fusion.3
  423.8 2.7 bitcast_dynamic-update-slice_fusion.2
  426.5 2.7 bitcast_dynamic-update-slice_fusion.1
  429.2 2.7 bitcast_dynamic-update-slice_fusion
  431.9 141.8 %all-to-all-done.2 = bf16[8,2,393216]{2,1,0:T(2,128)(2,1)} async-done(((bf16[8,2,393216]{2,1,0:T(2,128)(2,1)}), bf16[8,2,393216]{2,1,0:T(2,128)(2,1)}, u32[]{:S(2)}, u32[]{:S(2)}) %all-to-all-start.2) | async-done | bytes 12582944 | tf_op jit(solution)/shard_map/all_to_all | solution.py:57
  573.7 5.3 all-to-all-start.3
  579.1 0.2 reduce-scatter.3.cloned.1.call-start
  579.3 17.9 %reshape.43 = bf16[8192,1,768]{2,1,0:T(2,128)(2,1)} reshape(bf16[8,2,393216]{2,1,0:T(2,128)(2,1)} %all-to-all-done.1) | data formatting | bytes 25165824
  597.2 15.1 %copy.39 = bf16[1,768,8192]{1,2,0:T(8,128)(2,1)} copy(bf16[1,768,8192]{1,0,2:T(2,128)(2,1)} %bitcast.68) | data formatting | bytes 25165824
  612.3 16.6 %copy.33 = bf16[1,8,768,1024]{3,2,1,0:T(8,128)(2,1)} copy(bf16[1,8,768,1024]{2,3,1,0:T(8,128)(2,1)} %bitcast.70) | data formatting | bytes 25165824 | tf_op jit(solution)/shard_map/all_to_all | solution.py:56
  628.9 17.9 %reshape.41 = bf16[8192,1,768]{2,1,0:T(2,128)(2,1)} reshape(bf16[8,2,393216]{2,1,0:T(2,128)(2,1)} %all-to-all-done.2) | data formatting | bytes 25165824
  646.8 15.1 %copy.40 = bf16[1,768,8192]{1,2,0:T(8,128)(2,1)} copy(bf16[1,768,8192]{1,0,2:T(2,128)(2,1)} %bitcast.69) | data formatting | bytes 25165824
  661.9 16.6 %copy.35 = bf16[1,8,768,1024]{3,2,1,0:T(8,128)(2,1)} copy(bf16[1,8,768,1024]{2,3,1,0:T(8,128)(2,1)} %bitcast.71) | data formatting | bytes 25165824 | tf_op jit(solution)/shard_map/all_to_all | solution.py:57
  678.5 0.0 copy-start.7
  678.5 0.0 copy-start.8
  678.5 11.8 %fusion.4 = f32[512,1024]{1,0:T(8,128)S(1)} fusion(bf16[512,6144]{1,0:T(8,128)(2,1)} %all-gather.3.cloned.1.call-done, bf16[6144,1024]{1,0:T(8,128)(2,1)} %bitcast.72), kind=kOutput, calls=%fused_computation.34 | convolution fusion | flops 6442450944 | bytes 20971520 | tf_op jit(solution)/shard_map/dot_general | solution.py:68
  690.3 1.3 copy-done.13
  691.7 8.4 multiply_convert_fusion.2
  700.1 18.0 %all-to-all-done.3 = bf16[8,1,768,1024]{3,2,1,0:T(8,128)(2,1)} async-done(((bf16[8,1,768,1024]{3,2,1,0:T(8,128)(2,1)}), bf16[8,1,768,1024]{3,2,1,0:T(8,128)(2,1)}, u32[]{:S(2)}, u32[]{:S(2)}) %all-to-all-start.3) | async-done | bytes 12582944 | tf_op jit(solution)/shard_map/all_to_all | solution.py:59
  718.0 18.8 %convolution_convert_fusion = bf16[512,6144]{1,0:T(8,128)(2,1)} fusion(bf16[512,1024]{1,0:T(8,128)(2,1)S(1)} %get-tuple-element.14, bf16[6144,1024]{1,0:T(8,128)(2,1)} %bitcast.18), kind=kOutput, calls=%fused_computation.4 | convolution fusion | flops 6445596672 | bytes 19922944 | tf_op jit(solution)/shard_map/dot_general | solution.py:73
  736.9 0.0 reduce-scatter.3.cloned.1.call-update
  736.9 61.4 %reduce-scatter.3.cloned.1.call-done = bf16[512,768]{1,0:T(8,128)(2,1)} async-done(((bf16[512,6144]{1,0:T(8,128)(2,1)}), bf16[512,768]{1,0:T(8,128)(2,1)}) %reduce-scatter.3.cloned.1.call-update) | async-done | bytes 786448 | tf_op jit(solution)/shard_map/reduce_scatter | solution.py:85
  798.3 4.6 all-to-all-start.4
  802.9 19.9 %all-to-all-done.4 = bf16[4,128,768]{2,1,0:T(8,128)(2,1)S(1)} async-done(((bf16[4,128,768]{2,1,0:T(8,128)(2,1)}), bf16[4,128,768]{2,1,0:T(8,128)(2,1)S(1)}, u32[]{:S(2)}, u32[]{:S(2)}) %all-to-all-start.4) | async-done | bytes 786464 | tf_op jit(solution)/shard_map/all_to_all | solution.py:88
  822.8 1.0 fusion.1
  823.8 0.1 copy.38
  823.9 12.0 %psum.7 = f32[128,4]{0,1:T(4,128)S(1)} all-reduce(f32[128,4]{0,1:T(4,128)S(1)} %bitcast.82), channel_id=1, replica_groups=mesh['expert'=4,'tensor'=8] {'tensor'}, use_global_device_ids=true, to_apply=%region_6.0 | all-reduce | flops 512 | bytes 4096 | tf_op jit(solution)/shard_map/psum | solution.py:110
  835.9 1.0 multiply_convert_fusion.3
  836.9 23.4 %all_to_all.55 = bf16[4,128,768]{2,1,0:T(8,128)(2,1)} all-to-all(bf16[4,128,768]{2,1,0:T(8,128)(2,1)S(1)} %get-tuple-element.12), channel_id=1, replica_groups=mesh['expert'=4,'tensor'=8] {'expert'}, dimensions={0} | all-to-all | bytes 1572864 | tf_op jit(solution)/shard_map/all_to_all | solution.py:49
  860.2 0.0 all-gather.5.cloned.1.call-update
  860.3 0.0 reduce-scatter.5.cloned.1.call-start
  860.3 43.5 %all-gather.5.cloned.1.call-done = bf16[512,6144]{1,0:T(8,128)(2,1)} async-done(((bf16[512,768]{1,0:T(8,128)(2,1)}), bf16[512,6144]{1,0:T(8,128)(2,1)}) %all-gather.5.cloned.1.call-update) | async-done | bytes 6291472 | tf_op jit(solution)/shard_map/all_gather | solution.py:53
  903.8 14.5 %multiply_convert_fusion = (bf16[512,1024]{1,0:T(8,128)(2,1)S(1)}, bf16[512,1024]{1,0:T(8,128)(2,1)S(1)}) fusion(f32[1024]{0:T(1024)S(1)} %bitcast.87, f32[1024]{0:T(1024)S(1)} %bitcast.89, f32[512,1024]{1,0:T(8,128)} %copy-done.13, f32[1024]{0:T(1024)S(1)} %bitcast.91, f32[512,1024]{1,0:T(8,128)} %get-tuple-element.15, ...), kind=kOutput, calls=%fused_computation.5 | convolution fusion | flops 6451888128 | bytes 25178112 | tf_op jit(solution)/shard_map/dot_general | solution.py:75
  918.4 20.2 %fusion.5 = f32[512,6144]{1,0:T(8,128)} fusion(bf16[512,1024]{1,0:T(8,128)(2,1)S(1)} %get-tuple-element.11, bf16[6144,1024]{1,0:T(8,128)(2,1)} %bitcast.73), kind=kOutput, calls=%fused_computation.35 | convolution fusion | flops 6442450944 | bytes 26214400 | tf_op jit(solution)/shard_map/dot_general | solution.py:82
  938.6 20.3 %add_convert_fusion = bf16[512,6144]{1,0:T(8,128)(2,1)} fusion(f32[512,6144]{1,0:T(8,128)} %fusion.5, bf16[512,1024]{1,0:T(8,128)(2,1)S(1)} %get-tuple-element.10, bf16[6144,1024]{1,0:T(8,128)(2,1)} %bitcast.74), kind=kOutput, calls=%fused_computation.3 | convolution fusion | flops 6448742400 | bytes 32505856 | tf_op jit(solution)/shard_map/dot_general | solution.py:82
  958.8 0.0 reduce-scatter.5.cloned.1.call-update
  958.9 0.6 subtract_multiply_fusion
  959.5 12.5 %convert_bitcast_fusion.1 = bf16[1,6144,1024]{2,1,0:T(8,128)(2,1)} fusion(bf16[512,6144]{1,0:T(8,128)(2,1)} %all-gather.3.cloned.1.call-done, bf16[512,1024]{1,0:T(8,128)(2,1)} %copy-done.12), kind=kOutput, calls=%fused_computation.1 | convolution fusion | flops 6448742400 | bytes 19922944 | tf_op jit(solution)/shard_map/dot_general | solution.py:18
  972.0 9.8 convert_bitcast_fusion.2
  981.8 38.8 %reduce-scatter.5.cloned.1.call-done = bf16[512,768]{1,0:T(8,128)(2,1)} async-done(((bf16[512,6144]{1,0:T(8,128)(2,1)}), bf16[512,768]{1,0:T(8,128)(2,1)}) %reduce-scatter.5.cloned.1.call-update) | async-done | bytes 786448 | tf_op jit(solution)/shard_map/reduce_scatter | solution.py:95
  1020.6 4.6 all-to-all-start.6
  1025.2 11.8 %convert_bitcast_fusion = bf16[1,6144,1024]{2,1,0:T(8,128)(2,1)} fusion(bf16[512,6144]{1,0:T(8,128)(2,1)} %all-gather.5.cloned.1.call-done, bf16[512,1024]{1,0:T(8,128)(2,1)} %copy-done.11), kind=kOutput, calls=%fused_computation | convolution fusion | flops 6448742400 | bytes 19922944 | tf_op jit(solution)/shard_map/dot_general | solution.py:18
  1037.1 8.1 all-to-all-done.6
  1045.1 0.8 reduce_sum.60
  (37 shorter events, 0.2 us)
Async XLA Ops:
  9.8 197.2 %all-to-all-start = ((bf16[4,128,768]{2,1,0:T(8,128)(2,1)}), bf16[4,128,768]{2,1,0:T(8,128)(2,1)S(1)}, u32[]{:S(2)}, u32[]{:S(2)}) async-start(bf16[4,128,768]{2,1,0:T(8,128)(2,1)} %broadcast_multiply_fusion), calls=%async_computation | async-start | bytes 1572864 | tf_op jit(solution)/shard_map/all_to_all | solution.py:48
  207.0 0.9 copy-start.1
  207.9 196.3 %all-to-all-start.1 = ((bf16[8,2,393216]{2,1,0:T(2,128)(2,1)}), bf16[8,2,393216]{2,1,0:T(2,128)(2,1)}, u32[]{:S(2)}, u32[]{:S(2)}) async-start(bf16[8,2,393216]{2,1,0:T(2,128)(2,1)} %reshape.42), calls=%async_computation.1 | async-start | bytes 25165824 | tf_op jit(solution)/shard_map/all_to_all | solution.py:56
  404.1 169.6 %all-to-all-start.2 = ((bf16[8,2,393216]{2,1,0:T(2,128)(2,1)}), bf16[8,2,393216]{2,1,0:T(2,128)(2,1)}, u32[]{:S(2)}, u32[]{:S(2)}) async-start(bf16[8,2,393216]{2,1,0:T(2,128)(2,1)} %reshape.40), calls=%async_computation.2 | async-start | bytes 25165824 | tf_op jit(solution)/shard_map/all_to_all | solution.py:57
  409.5 269.0 %all-gather.3.cloned.1.call-start = ((), (), s32[]{:S(2)}) async-start(), calls=%async_computation.9 | async-start | bytes 7077888 | tf_op jit(solution)/shard_map/all_gather | solution.py:52
  573.7 144.3 %all-to-all-start.3 = ((bf16[8,1,768,1024]{3,2,1,0:T(8,128)(2,1)}), bf16[8,1,768,1024]{3,2,1,0:T(8,128)(2,1)}, u32[]{:S(2)}, u32[]{:S(2)}) async-start(bf16[8,1,768,1024]{3,2,1,0:T(8,128)(2,1)} %bitcast_dynamic-update-slice_fusion), calls=%async_computation.3 | async-start | bytes 25165824 | tf_op jit(solution)/shard_map/all_to_all | solution.py:59
  579.1 219.2 %reduce-scatter.3.cloned.1.call-start = ((), (), s32[]{:S(2)}) async-start(), calls=%async_computation.10 | async-start | bytes 7077888 | tf_op jit(solution)/shard_map/reduce_scatter | solution.py:85
  678.5 13.2 %copy-start = (bf16[1,8,768,1024]{3,2,1,0:T(8,128)(2,1)S(1)}, bf16[1,8,768,1024]{3,2,1,0:T(8,128)(2,1)}, u32[]{:S(2)}) copy-start(bf16[1,8,768,1024]{3,2,1,0:T(8,128)(2,1)} %copy.35) | copy-start | bytes 37748740
  678.5 13.2 %copy-start.5 = (bf16[512,6144]{1,0:T(8,128)(2,1)S(1)}, bf16[512,6144]{1,0:T(8,128)(2,1)}, u32[]{:S(2)}) copy-start(bf16[512,6144]{1,0:T(8,128)(2,1)} %all-gather.3.cloned.1.call-done) | copy-start | bytes 18874372
  678.5 13.2 %copy-start.6 = (f32[1,1024]{1,0:T(1,128)S(1)}, f32[1,1024]{1,0:T(1,128)}, u32[]{:S(2)}) copy-start(f32[1,1024]{1,0:T(1,128)} %param.19) | copy-start | bytes 12292
  678.5 13.2 %copy-start.7 = (f32[1,1024]{1,0:T(1,128)S(1)}, f32[1,1024]{1,0:T(1,128)}, u32[]{:S(2)}) copy-start(f32[1,1024]{1,0:T(1,128)} %param.18) | copy-start | bytes 12292
  678.5 13.2 %copy-start.8 = (f32[1,1024]{1,0:T(1,128)S(1)}, f32[1,1024]{1,0:T(1,128)}, u32[]{:S(2)}) copy-start(f32[1,1024]{1,0:T(1,128)} %param.17) | copy-start | bytes 12292
  690.3 1.3 copy-start.13
  700.1 36.8 %copy-start.11 = (bf16[512,1024]{1,0:T(8,128)(2,1)}, bf16[512,1024]{1,0:T(8,128)(2,1)S(1)}, u32[]{:S(2)}) copy-start(bf16[512,1024]{1,0:T(8,128)(2,1)S(1)} %get-tuple-element.14) | copy-start | bytes 3145732
  718.0 84.8 %copy-start.2 = (bf16[128,768]{1,0:T(8,128)(2,1)S(1)}, bf16[128,768]{1,0:T(8,128)(2,1)}, u32[]{:S(2)}) copy-start(bf16[128,768]{1,0:T(8,128)(2,1)} %param.11) | copy-start | bytes 589828
  718.0 84.9 %copy-start.4 = (f32[128,2]{0,1:T(2,128)S(1)}, f32[128,2]{0,1:T(2,128)}, u32[]{:S(2)}) copy-start(f32[128,2]{0,1:T(2,128)} %param.13) | copy-start | bytes 3076
  736.9 99.0 %copy-start.3 = (s32[128,2]{0,1:T(2,128)S(1)}, s32[128,2]{0,1:T(2,128)}, u32[]{:S(2)}) copy-start(s32[128,2]{0,1:T(2,128)} %param.12) | copy-start | bytes 3076
  798.3 24.5 %all-to-all-start.4 = ((bf16[4,128,768]{2,1,0:T(8,128)(2,1)}), bf16[4,128,768]{2,1,0:T(8,128)(2,1)S(1)}, u32[]{:S(2)}, u32[]{:S(2)}) async-start(bf16[4,128,768]{2,1,0:T(8,128)(2,1)} %bitcast.79), calls=%async_computation.5 | async-start | bytes 1572864 | tf_op jit(solution)/shard_map/all_to_all | solution.py:88
  802.9 100.9 %all-gather.5.cloned.1.call-start = ((), (), s32[]{:S(2)}) async-start(), calls=%async_computation.11 | async-start | bytes 7077888 | tf_op jit(solution)/shard_map/all_gather | solution.py:53
  860.3 160.3 %reduce-scatter.5.cloned.1.call-start = ((), (), s32[]{:S(2)}) async-start(), calls=%async_computation.12 | async-start | bytes 7077888 | tf_op jit(solution)/shard_map/reduce_scatter | solution.py:95
  918.3 20.2 %copy-start.9 = (bf16[512,1024]{1,0:T(8,128)(2,1)}, bf16[512,1024]{1,0:T(8,128)(2,1)S(1)}, u32[]{:S(2)}) copy-start(bf16[512,1024]{1,0:T(8,128)(2,1)S(1)} %get-tuple-element.11) | copy-start | bytes 3145732
  918.4 20.2 %copy-start.12 = (bf16[512,1024]{1,0:T(8,128)(2,1)}, bf16[512,1024]{1,0:T(8,128)(2,1)S(1)}, u32[]{:S(2)}) copy-start(bf16[512,1024]{1,0:T(8,128)(2,1)S(1)} %get-tuple-element.10) | copy-start | bytes 3145732
  958.8 13.2 %slice-start = ((s8[6291456]{0:T(1024)(128)(4,1)}), s8[2097152]{0:T(1024)(128)(4,1)S(1)}, s32[]{:S(2)}) async-start(s8[6291456]{0:T(1024)(128)(4,1)} %bitcast.84), calls=%async_computation.13 | async-start | bytes 4194304
  959.5 12.5 %slice-start.1 = ((s8[6291456]{0:T(1024)(128)(4,1)}), s8[4194304]{0:T(1024)(128)(4,1)S(1)}, s32[]{:S(2)}) async-start(s8[6291456]{0:T(1024)(128)(4,1)} %bitcast.84), calls=%async_computation.14 | async-start | bytes 8388608
  959.5 12.5 %copy-start.10 = (bf16[512,1024]{1,0:T(8,128)(2,1)S(1)}, bf16[512,1024]{1,0:T(8,128)(2,1)}, u32[]{:S(2)}) copy-start(bf16[512,1024]{1,0:T(8,128)(2,1)} %copy-done.9) | copy-start | bytes 3145732
  1020.6 24.5 %all-to-all-start.6 = ((bf16[4,128,768]{2,1,0:T(8,128)(2,1)}), bf16[4,128,768]{2,1,0:T(8,128)(2,1)S(1)}, u32[]{:S(2)}, u32[]{:S(2)}) async-start(bf16[4,128,768]{2,1,0:T(8,128)(2,1)} %bitcast.78), calls=%async_computation.8 | async-start | bytes 1572864 | tf_op jit(solution)/shard_map/all_to_all | solution.py:98
Sparse Core Ops, SparseCore 0:
  412.2 112.5 all-gather.2
  737.0 61.2 reduce-scatter.2
  860.4 43.3 all-gather.4
  959.0 61.5 reduce-scatter.4
